TPU v7x, 256 devices: a whole 4x4x8 slice. The times are simulated.
256 devices in a mesh: blk: 32 (over x_lo, z, core), tp: 8 (over x_hi, y).
Axes of the slice: x: 4 (x_hi: 2, x_lo: 2; x = x_hi * 2 + x_lo), y: 4, z: 8, core: 2. Of those that a mesh axis runs over, the one named last changes fastest.
Arguments:
- tokens: bfloat16 [8192, 8192], P('blk', 'tp'), may hold values from -6 to 6
- weight: bfloat16 [8192, 2048], P('tp'), may hold values from -0.0625 to 0.0625
- bank_a: bfloat16 [32, 8192, 32], P('blk', 'tp'), may hold values from -0.0625 to 0.0625
- bank_b: bfloat16 [32, 32, 1024], P('blk'), may hold values from -1.5 to 1.5
- tile_map: int32 [64, 1], P('blk'), may hold values from 0 to 31
- grad_out: bfloat16 [8192, 2048], P(('blk', 'tp')), may hold values from -6 to 6
Outputs:
- key_value_output: bfloat16 [8192, 2048], P(('blk', 'tp'))
- token_gradient: bfloat16 [8192, 8192], P('blk', 'tp')
- grad_a: float32 [32, 8192, 32], P('blk', 'tp')
- grad_b: float32 [32, 32, 1024], P('blk', None, 'tp')
Inputs may be any that keep to these rules, and one draw needn't show every extreme that they name: `tile_map`: every one of the 32 adapters is the adapter of at least one tile.
All inputs are finite; a program needn't handle non-finite values.
Results may differ from a plain program's by a relative error of at most 0.003.
Values may be sent and summed in bfloat16 or wider, within the bound.
A program may use at most 64 MiB of HBM per device.

v0:
```python
import jax
import jax.numpy as jnp
from jax import lax
from jax.sharding import PartitionSpec as P

adapter_scale = 0.5


def on_device(tokens, weight, bank_a, bank_b, tile_map, grad_out):
    f32, bf16 = (jnp.float32, jnp.bfloat16)
    tile_ids = tile_map[:, 0]
    rows, feats = tokens.shape
    tiles = tile_ids.shape[0]
    tile_rows = rows // tiles
    rank_two = bank_a.shape[2]
    rank_one = rank_two // 2
    kv_width = bank_b.shape[2]
    tp_count = lax.axis_size("tp")
    tp_id = lax.axis_index("tp")
    kv_dev = kv_width // tp_count
    col0 = tp_id * kv_dev
    b_cols = lax.dynamic_slice_in_dim(bank_b, col0, kv_dev, 2)
    all_b = lax.all_gather(b_cols, "blk", axis=0, tiled=True)
    all_a = lax.all_gather(bank_a, "blk", axis=0, tiled=True)
    grad_rows = lax.all_gather(grad_out, "tp", axis=0, tiled=True)
    fac_a = jnp.stack([all_a[tile_ids[t]] for t in range(tiles)])
    fac_b = jnp.stack([all_b[tile_ids[t]] for t in range(tiles)])
    tok_t = tokens.reshape(tiles, tile_rows, feats)
    g_t = grad_rows.reshape(tiles, tile_rows, 2 * kv_width)
    g_key = lax.dynamic_slice_in_dim(g_t, col0, kv_dev, 2)
    g_val = lax.dynamic_slice_in_dim(g_t, kv_width + col0, kv_dev, 2)
    act_part = jnp.einsum("tre,tek->trk", tok_t, fac_a, preferred_element_type=f32)
    grad_part = jnp.concatenate(
        [
            jnp.einsum("trc,tkc->trk", g_key, fac_b[:, :rank_one], preferred_element_type=f32),
            jnp.einsum("trc,tkc->trk", g_val, fac_b[:, rank_one:], preferred_element_type=f32),
        ],
        axis=2,
    )
    both = lax.psum(jnp.stack([act_part, grad_part]), "tp")
    rank_act = both[0].astype(bf16)
    rank_grad = both[1].astype(bf16)
    lora_key = jnp.einsum(
        "trk,tkc->trc", rank_act[:, :, :rank_one], fac_b[:, :rank_one], preferred_element_type=f32
    ).reshape(rows, kv_dev)
    lora_val = jnp.einsum(
        "trk,tkc->trc", rank_act[:, :, rank_one:], fac_b[:, rank_one:], preferred_element_type=f32
    ).reshape(rows, kv_dev)
    base = jnp.dot(tokens, weight, preferred_element_type=f32)
    base = lax.dynamic_update_slice_in_dim(
        base, lax.dynamic_slice_in_dim(base, col0, kv_dev, 1) + adapter_scale * lora_key, col0, 1
    )
    base = lax.dynamic_update_slice_in_dim(
        base,
        lax.dynamic_slice_in_dim(base, kv_width + col0, kv_dev, 1) + adapter_scale * lora_val,
        kv_width + col0,
        1,
    )
    key_value_output = lax.psum_scatter(base, "tp", scatter_dimension=0, tiled=True).astype(bf16)
    backward = jnp.dot(grad_rows, weight.T, preferred_element_type=f32)
    adapter_back = jnp.einsum("tru,tyu->try", rank_grad, fac_a, preferred_element_type=f32)
    token_gradient = (backward + adapter_scale * adapter_back.reshape(rows, feats)).astype(bf16)
    down_grad = adapter_scale * jnp.einsum(
        "tre,trk->tek", tok_t, rank_grad, preferred_element_type=f32
    )
    up_grad = adapter_scale * jnp.concatenate(
        [
            jnp.einsum(
                "trk,trc->tkc", rank_act[:, :, :rank_one], g_key, preferred_element_type=f32
            ),
            jnp.einsum(
                "trk,trc->tkc", rank_act[:, :, rank_one:], g_val, preferred_element_type=f32
            ),
        ],
        axis=1,
    )
    size_a = feats * rank_two
    flat = jnp.concatenate([down_grad.reshape(tiles, -1), up_grad.reshape(tiles, -1)], axis=1)
    adapters = bank_a.shape[0] * lax.axis_size("blk")
    one_hot = (tile_ids[:, None] == jnp.arange(adapters, dtype=jnp.int32)[None, :]).astype(f32)
    dense = jnp.dot(one_hot.T, flat, precision=lax.Precision.HIGHEST, preferred_element_type=f32)
    summed = lax.psum_scatter(
        dense.reshape(adapters, -1, 128), "blk", scatter_dimension=0, tiled=True
    ).reshape(bank_a.shape[0], -1)
    grad_a = summed[:, :size_a].reshape(bank_a.shape[0], feats, rank_two)
    grad_b = summed[:, size_a:].reshape(bank_a.shape[0], rank_two, kv_dev)
    return (key_value_output, token_gradient, grad_a, grad_b)


def solution(mesh):
    in_specs = (
        P("blk", "tp"),
        P("tp", None),
        P("blk", "tp", None),
        P("blk", None, None),
        P("blk", None),
        P(("blk", "tp"), None),
    )
    out_specs = (P(("blk", "tp"), None), P("blk", "tp"), P("blk", "tp", None), P("blk", None, "tp"))
    return jax.shard_map(
        on_device, mesh=mesh, in_specs=in_specs, out_specs=out_specs, check_vma=False
    )
```

profile of v0, /device:TPU:8, one launch (start us, length us, event | category | flops | bytes accessed | tf_op | source)
XLA Modules:
  0.0 386.3 jit_solution(8638338468976449265)
XLA Ops:
  7.2 0.7 all-gather.5.cloned.1.call-update
  8.0 0.7 all-gather.3.cloned.1.call-update
  8.7 1.3 fusion.33
  13.9 0.7 constant_dynamic-slice_fusion.2
  14.6 38.0 %all_gather.11 = bf16[32,32,128]{2,1,0:T(8,128)(2,1)S(1)} all-gather(bf16[1,32,128]{2,1,0:T(8,128)(2,1)S(1)} %constant_dynamic-slice_fusion.2), channel_id=1, replica_groups=mesh['blk'=32,'tp'=8] {'blk'}, dimensions={0}, use_global_device_ids=true | all-gather | bytes 270336 | tf_op jit(solution)/shard_map/all_gather | solution.py:23
  52.6 3.4 fusion.34
  56.1 8.7 %all-gather.5.cloned.1.call-done = bf16[256,2048]{1,0:T(8,128)(2,1)} async-done(((bf16[32,2048]{1,0:T(8,128)(2,1)}), bf16[256,2048]{1,0:T(8,128)(2,1)}) %all-gather.5.cloned.1.call-update) | async-done | bytes 1048592 | tf_op jit(solution)/shard_map/all_gather | solution.py:25
  64.8 1.0 fusion.7
  65.8 1.0 fusion.11
  66.8 63.7 %all-gather.3.cloned.1.call-done = bf16[32,1024,32]{1,2,0:T(8,128)(2,1)} async-done(((bf16[1,1024,32]{1,2,0:T(8,128)(2,1)}), bf16[32,1024,32]{1,2,0:T(8,128)(2,1)}) %all-gather.3.cloned.1.call-update) | async-done | bytes 2097168 | tf_op jit(solution)/shard_map/all_gather | solution.py:24
  130.4 0.9 constant_dynamic-slice_fusion.4
  131.3 0.3 convolution_bitcast_fusion.1
  131.6 36.5 %psum.7 = bf16[2,2,128,32]{2,3,1,0:T(8,128)(2,1)S(1)} all-reduce(f32[2,2,128,32]{2,3,1,0:T(8,128)S(1)} %pad_maximum_fusion.3), channel_id=1, replica_groups=mesh['blk'=32,'tp'=8] {'tp'}, use_global_device_ids=true, to_apply=%region_0.0 | all-reduce | flops 16384 | bytes 98304 | tf_op jit(solution)/shard_map/psum | solution.py:40
  168.2 0.2 convolution_multiply_fusion.2
  168.4 0.2 convolution_multiply_fusion.3
  168.7 1.4 copy-done.1
  170.2 1.0 fusion.9
  171.1 1.0 fusion.5
  172.2 0.2 fusion.1
  172.4 0.3 copy.12
  172.7 0.6 reshape.50
  173.3 2.2 convolution_bitcast_fusion
  175.5 3.0 copy.15
  178.5 0.3 convolution_multiply_fusion
  178.8 0.8 copy-done.2
  179.7 4.3 %fusion = bf16[256,1024]{1,0:T(8,128)(2,1)} fusion(f32[256,1024]{1,0:T(8,128)S(1)} %bitcast.43, bf16[256,2048]{1,0:T(8,128)(2,1)S(1)} %copy-done.2, bf16[1024,2048]{1,0:T(8,128)(2,1)} %param.7), kind=kOutput, calls=%fused_computation.3 | convolution fusion | flops 1074266112 | bytes 6815744 | tf_op jit(solution)/shard_map/dot_general | solution.py:60
  183.9 67.5 %reduce-scatter.3.cloned.1.call-done = f32[32,2048]{1,0:T(8,128)} async-done(((f32[256,2048]{1,0:T(8,128)}), f32[32,2048]{1,0:T(8,128)}) %reduce-scatter.3.cloned.1.call-update) | async-done | bytes 262160 | tf_op jit(solution)/shard_map/reduce_scatter | solution.py:59
  251.5 1.6 convert_element_type.16
  253.1 123.1 %reduce-scatter.5.cloned.1.call-done = f32[1,288,128]{2,1,0:T(8,128)} async-done(((f32[32,288,128]{2,1,0:T(8,128)}), f32[1,288,128]{2,1,0:T(8,128)}) %reduce-scatter.5.cloned.1.call-update) | async-done | bytes 147472 | tf_op jit(solution)/shard_map/reduce_scatter | solution.py:82
  376.2 1.3 slice.57
  377.5 1.2 slice_reduce_fusion
  378.9 0.8 copy.13
  (21 shorter events, 0.5 us)
Async XLA Ops:
  7.2 45.5 %copy-start = (bf16[256,1024]{1,0:T(8,128)(2,1)S(1)}, bf16[256,1024]{1,0:T(8,128)(2,1)}, u32[]{:S(2)}) copy-start(bf16[256,1024]{1,0:T(8,128)(2,1)} %param.6) | copy-start | bytes 1572868
  7.2 57.6 %all-gather.5.cloned.1.call-start = ((), (), s32[]{:S(2)}) async-start(), calls=%async_computation.3 | async-start | bytes 1179648 | tf_op jit(solution)/shard_map/all_gather | solution.py:25
  7.9 122.5 %all-gather.3.cloned.1.call-start = ((), (), s32[]{:S(2)}) async-start(), calls=%async_computation.2 | async-start | bytes 2162688 | tf_op jit(solution)/shard_map/all_gather | solution.py:24
  8.7 242.8 %reduce-scatter.3.cloned.1.call-start = ((), (), s32[]{:S(2)}) async-start(), calls=%async_computation.4 | async-start | bytes 2359296 | tf_op jit(solution)/shard_map/reduce_scatter | solution.py:59
  64.8 108.5 %copy-start.3 = (s32[2,1]{0,1:T(1,128)S(1)}, s32[2,1]{0,1:T(1,128)}, u32[]{:S(2)}) copy-start(s32[2,1]{0,1:T(1,128)} %param.10) | copy-start | bytes 28
  168.7 1.4 copy-start.1
  170.1 206.0 %reduce-scatter.5.cloned.1.call-start = ((), (), s32[]{:S(2)}) async-start(), calls=%async_computation.5 | async-start | bytes 4866048 | tf_op jit(solution)/shard_map/reduce_scatter | solution.py:82
  178.4 1.2 copy-start.2
Sparse Core Ops, SparseCore 0:
  10.7 54.0 all-gather.4
  66.7 63.7 all-gather.2
  170.2 81.1 reduce-scatter.2
  253.9 122.2 reduce-scatter.4
where the time goes:
time: 387 us; the launch traced here: 386 us
  waiting for transfers between devices  264 us (68%)
  blocking collectives  74.6 us (19%)
  between operations  17.8 us (5%)
  matrix products  15 us (4%)
  local copies, waits for them, and re-layouts  12.6 us (3%)
    reduce_scatter x1, waiting for transfers between devices, on_device(): lax.psum_scatter(dense.reshape(adapters, -1, 128), 'blk', scatter_dimensi...  123 us
    reduce_scatter x1, waiting for transfers between devices, on_device(): lax.psum_scatter(base, 'tp', scatter_dimension=0, tiled=True).astype(bf16)  67.5 us
    all_gather x1, waiting for transfers between devices, on_device(): all_a = lax.all_gather(bank_a, 'blk', axis=0, tiled=True)  63.7 us
    all_gather x1, blocking collectives, on_device(): all_b = lax.all_gather(b_cols, 'blk', axis=0, tiled=True)  38 us
    psum x1, blocking collectives, on_device(): both = lax.psum(jnp.stack([act_part, grad_part]), 'tp')  36.5 us
    all_gather x1, waiting for transfers between devices, on_device(): grad_rows = lax.all_gather(grad_out, 'tp', axis=0, tiled=True)  8.72 us
  transfers between devices with their start and end apart: 4, of which 4 were waited for; matrix products, arithmetic and copies ran while one was open for 6% of the time, Pallas kernels for 0%

commit v1 on v0

--- a/solution.py
+++ b/solution.py
@@ -22,7 +22,9 @@
     b_cols = lax.dynamic_slice_in_dim(bank_b, col0, kv_dev, 2)
     all_b = lax.all_gather(b_cols, "blk", axis=0, tiled=True)
     all_a = lax.all_gather(bank_a, "blk", axis=0, tiled=True)
-    grad_rows = lax.all_gather(grad_out, "tp", axis=0, tiled=True)
+    passed = jnp.stack([grad_out for _ in range(lax.axis_size("tp"))], axis=0)
+    tile_out = lax.all_to_all(passed, "tp", 0, 0)
+    grad_rows = jnp.concatenate(tile_out, axis=0)
     fac_a = jnp.stack([all_a[tile_ids[t]] for t in range(tiles)])
     fac_b = jnp.stack([all_b[tile_ids[t]] for t in range(tiles)])
     tok_t = tokens.reshape(tiles, tile_rows, feats)

time: 387 us -> 334 us (0.86)
  waiting for transfers between devices: 264 us -> 204 us
  starting transfers between devices: 0.16 us -> 7.46 us
    all_gather x1, waiting for transfers between devices: 63.7 us -> 11.8 us  [on_device(): all_a = lax.all_gather(bank_a, 'blk', axis=0, tiled=True)]
    all_gather x1 -> x0, waiting for transfers between devices: 8.72 us -> none  [on_device(): grad_rows = lax.all_gather(grad_out, 'tp', axis=0, tiled=True)]
    all_to_all x0 -> x1, starting transfers between devices: none -> 7.38 us  [on_device(): tile_out = lax.all_to_all(passed, 'tp', 0, 0)]
  transfers between devices with their start and end apart: 4 -> 4, of which waited for: 4 -> 3; matrix products, arithmetic and copies ran while one was open for 6% -> 7% of each run, Pallas kernels for 0% -> 0%
where the time goes in v1:
time: 334 us; the launch traced here: 333 us
  waiting for transfers between devices  204 us (61%)
  blocking collectives  73.6 us (22%)
  between operations  17.8 us (5%)
  matrix products  15.4 us (5%)
  local copies, waits for them, and re-layouts  13.8 us (4%)
  starting transfers between devices  7.46 us (2%)
    reduce_scatter x1, waiting for transfers between devices, on_device(): lax.psum_scatter(dense.reshape(adapters, -1, 128), 'blk', scatter_dimensi...  123 us
    reduce_scatter x1, waiting for transfers between devices, on_device(): lax.psum_scatter(base, 'tp', scatter_dimension=0, tiled=True).astype(bf16)  68 us
    all_gather x1, blocking collectives, on_device(): all_b = lax.all_gather(b_cols, 'blk', axis=0, tiled=True)  37 us
    psum x1, blocking collectives, on_device(): both = lax.psum(jnp.stack([act_part, grad_part]), 'tp')  36.6 us
    all_gather x1, waiting for transfers between devices, on_device(): all_a = lax.all_gather(bank_a, 'blk', axis=0, tiled=True)  11.8 us
    all_to_all x1, starting transfers between devices, on_device(): tile_out = lax.all_to_all(passed, 'tp', 0, 0)  7.38 us
  transfers between devices with their start and end apart: 4, of which 3 were waited for; matrix products, arithmetic and copies ran while one was open for 7% of the time, Pallas kernels for 0%

profile of v1, /device:TPU:8, one launch (start us, length us, event | category | flops | bytes accessed | tf_op | source)
XLA Modules:
  0.0 333.4 jit_solution(10787583234750047959)
XLA Ops:
  7.2 0.7 all-gather.2.cloned.1.call-update
  7.9 2.0 stack.28
  9.9 7.4 %all-to-all-start = ((bf16[8,32,2048]{2,1,0:T(8,128)(2,1)}), bf16[8,32,2048]{2,1,0:T(8,128)(2,1)}, u32[]{:S(2)}, u32[]{:S(2)}) async-start(bf16[8,32,2048]{2,1,0:T(8,128)(2,1)} %stack.28), calls=%async_computation | async-start | bytes 2097152 | tf_op jit(solution)/shard_map/all_to_all | solution.py:26
  17.3 1.3 fusion.33
  22.5 0.7 constant_dynamic-slice_fusion.2
  23.2 37.0 %all_gather.7 = bf16[32,32,128]{2,1,0:T(8,128)(2,1)S(1)} all-gather(bf16[1,32,128]{2,1,0:T(8,128)(2,1)S(1)} %constant_dynamic-slice_fusion.2), channel_id=1, replica_groups=mesh['blk'=32,'tp'=8] {'blk'}, dimensions={0}, use_global_device_ids=true | all-gather | bytes 270336 | tf_op jit(solution)/shard_map/all_gather | solution.py:23
  60.2 3.5 %fusion.34 = f32[256,2048]{1,0:T(8,128)S(1)} fusion(bf16[256,1024]{1,0:T(8,128)(2,1)S(1)} %copy-done, bf16[1024,2048]{1,0:T(8,128)(2,1)} %param.7), kind=kOutput, calls=%fused_computation.59 | convolution fusion | flops 1073741824 | bytes 6815744 | tf_op jit(solution)/shard_map/dot_general | solution.py:51
  63.7 1.0 fusion.7
  64.7 1.0 fusion.11
  65.7 11.8 %all-gather.2.cloned.1.call-done = bf16[32,1024,32]{1,2,0:T(8,128)(2,1)} async-done(((bf16[1,1024,32]{1,2,0:T(8,128)(2,1)}), bf16[32,1024,32]{1,2,0:T(8,128)(2,1)}) %all-gather.2.cloned.1.call-update) | async-done | bytes 2097168 | tf_op jit(solution)/shard_map/all_gather | solution.py:24
  77.5 0.9 constant_dynamic-slice_fusion.4
  78.4 0.3 convolution_bitcast_fusion.1
  78.7 36.6 %psum.7 = bf16[2,2,128,32]{2,3,1,0:T(8,128)(2,1)S(1)} all-reduce(f32[2,2,128,32]{2,3,1,0:T(8,128)S(1)} %pad_maximum_fusion.3), channel_id=1, replica_groups=mesh['blk'=32,'tp'=8] {'tp'}, use_global_device_ids=true, to_apply=%region_0.0 | all-reduce | flops 16384 | bytes 98304 | tf_op jit(solution)/shard_map/psum | solution.py:42
  115.3 0.2 convolution_multiply_fusion.2
  115.5 0.2 convolution_multiply_fusion.3
  115.8 1.4 copy-done.1
  117.2 1.0 fusion.9
  118.2 1.0 fusion.5
  119.2 0.2 fusion.1
  119.4 0.3 copy.12
  119.8 0.6 reshape.52
  120.4 2.1 convolution_bitcast_fusion
  122.5 3.0 copy.15
  125.5 0.3 convolution_multiply_fusion
  125.9 4.6 %fusion = bf16[256,1024]{1,0:T(8,128)(2,1)} fusion(f32[256,1024]{1,0:T(8,128)S(1)} %bitcast.44, bf16[256,2048]{1,0:T(8,128)(2,1)} %bitcast.10, bf16[1024,2048]{1,0:T(8,128)(2,1)} %param.7), kind=kOutput, calls=%fused_computation.3 | convolution fusion | flops 1074266112 | bytes 6815744 | tf_op jit(solution)/shard_map/dot_general | solution.py:62
  130.5 68.0 %reduce-scatter.3.cloned.1.call-done = f32[32,2048]{1,0:T(8,128)} async-done(((f32[256,2048]{1,0:T(8,128)}), f32[32,2048]{1,0:T(8,128)}) %reduce-scatter.3.cloned.1.call-update) | async-done | bytes 262160 | tf_op jit(solution)/shard_map/reduce_scatter | solution.py:61
  198.5 1.6 convert_element_type.16
  200.1 123.2 %reduce-scatter.5.cloned.1.call-done = f32[1,288,128]{2,1,0:T(8,128)} async-done(((f32[32,288,128]{2,1,0:T(8,128)}), f32[1,288,128]{2,1,0:T(8,128)}) %reduce-scatter.5.cloned.1.call-update) | async-done | bytes 147472 | tf_op jit(solution)/shard_map/reduce_scatter | solution.py:84
  323.3 1.3 slice.57
  324.7 1.2 slice_reduce_fusion
  325.9 0.2 reshape.55
  326.1 0.8 copy.13
  (19 shorter events, 0.3 us)
Async XLA Ops:
  7.2 53.1 %copy-start = (bf16[256,1024]{1,0:T(8,128)(2,1)S(1)}, bf16[256,1024]{1,0:T(8,128)(2,1)}, u32[]{:S(2)}) copy-start(bf16[256,1024]{1,0:T(8,128)(2,1)} %param.6) | copy-start | bytes 1572868
  7.2 70.3 %all-gather.2.cloned.1.call-start = ((), (), s32[]{:S(2)}) async-start(), calls=%async_computation.3 | async-start | bytes 2162688 | tf_op jit(solution)/shard_map/all_gather | solution.py:24
  9.9 53.8 %all-to-all-start = ((bf16[8,32,2048]{2,1,0:T(8,128)(2,1)}), bf16[8,32,2048]{2,1,0:T(8,128)(2,1)}, u32[]{:S(2)}, u32[]{:S(2)}) async-start(bf16[8,32,2048]{2,1,0:T(8,128)(2,1)} %stack.28), calls=%async_computation | async-start | bytes 2097152 | tf_op jit(solution)/shard_map/all_to_all | solution.py:26
  17.3 181.2 %reduce-scatter.3.cloned.1.call-start = ((), (), s32[]{:S(2)}) async-start(), calls=%async_computation.4 | async-start | bytes 2359296 | tf_op jit(solution)/shard_map/reduce_scatter | solution.py:61
  63.7 56.6 %copy-start.2 = (s32[2,1]{0,1:T(1,128)S(1)}, s32[2,1]{0,1:T(1,128)}, u32[]{:S(2)}) copy-start(s32[2,1]{0,1:T(1,128)} %param.10) | copy-start | bytes 28
  115.8 1.4 copy-start.1
  117.2 206.1 %reduce-scatter.5.cloned.1.call-start = ((), (), s32[]{:S(2)}) async-start(), calls=%async_computation.5 | async-start | bytes 4866048 | tf_op jit(solution)/shard_map/reduce_scatter | solution.py:84
Sparse Core Ops, SparseCore 0:
  9.9 67.5 all-gather.1
  117.3 81.1 reduce-scatter.2
  201.0 122.2 reduce-scatter.4
